TPU v7x, 256 devices: a whole 4x4x8 slice. The times are simulated.
256 devices in a mesh: phase: 8 (over y, x_hi), slab: 32 (over x_lo, z, core).
Axes of the slice: x: 4 (x_hi: 2, x_lo: 2; x = x_hi * 2 + x_lo), y: 4, z: 8, core: 2. Of those that a mesh axis runs over, the one named last changes fastest.
Arguments:
- images: float32 [16, 1024, 64, 128], P('phase', 'slab'), may hold values from -8 to 8, as said below
Outputs:
- forces: float32 [3, 16, 1024, 64, 128], P(None, 'phase', 'slab')
Inputs may be any that keep to these rules, and one draw needn't show every extreme that they name: `images`: Breathing-phase volumes of one body.
All inputs are finite; a program needn't handle non-finite values.
Results may differ from a plain program's by a relative error of at most 0.0001.
Values sent between devices are 32-bit elements; how exact they have to be, the bound alone decides.
A program may use at most 128 MiB of HBM per device.

v0:
```python
import jax
import jax.numpy as jnp
from jax import lax
from jax.sharding import PartitionSpec as P

EPSILON = 1e-05


def padded_2(array, sides, width):
    for axis, dim in sides:
        size, length = (lax.axis_size(axis), array.shape[dim])
        up = [(i, (i + 1) % size) for i in range(size - 1)]
        down = [(j, i) for i, j in up]
        last = lax.slice_in_dim(array, length - width, length, axis=dim)
        first = lax.slice_in_dim(array, 0, width, axis=dim)
        before = lax.ppermute(last, axis, up)
        after = lax.ppermute(first, axis, down)
        array = jnp.concatenate([before, array, after], axis=dim)
    return array


def passed_along(value, axis, steps):
    count = lax.axis_size(axis)
    pairs = [(source, (source + steps) % count) for source in range(count)]
    return lax.ppermute(value, axis, pairs)


def window_mean(field):
    inner_depth = field.shape[0] - 8
    summed = sum((field[offset : offset + inner_depth] for offset in range(9)))
    for direction in (1, 2):
        widths = [(4, 4) if dimension == direction else (0, 0) for dimension in range(3)]
        padded = jnp.pad(summed, widths)
        length = summed.shape[direction]
        summed = sum(
            (
                lax.slice_in_dim(padded, offset, offset + length, axis=direction)
                for offset in range(9)
            )
        )
    return summed / 729.0


def phase_stats(rimmed):
    mean_field = window_mean(rimmed)
    spread = window_mean(rimmed * rimmed) - mean_field * mean_field
    offset_field = rimmed[4:-4] - mean_field
    return (rimmed, mean_field, spread, offset_field)


def pair_terms(left_stats, right_stats):
    left_rimmed, mean_left, spread_left, offset_left = left_stats
    right_rimmed, mean_right, spread_right, offset_right = right_stats
    covariance = window_mean(left_rimmed * right_rimmed) - mean_left * mean_right
    weight = 2.0 * covariance / (spread_left * spread_right + EPSILON)
    toward_left = weight * (offset_right - covariance / (spread_left + EPSILON) * offset_left)
    toward_right = weight * (offset_left - covariance / (spread_right + EPSILON) * offset_right)
    return (toward_left, toward_right)


def gradient(rimmed):
    inner_depth = rimmed.shape[0] - 8
    core = rimmed[4 : 4 + inner_depth]
    along_z = (rimmed[5 : 5 + inner_depth] - rimmed[3 : 3 + inner_depth]) * 0.5
    padded = jnp.pad(core, ((0, 0), (1, 1), (1, 1)))
    along_y = (padded[:, 2:, 1:-1] - padded[:, :-2, 1:-1]) * 0.5
    along_x = (padded[:, 1:-1, 2:] - padded[:, 1:-1, :-2]) * 0.5
    return jnp.stack([along_z, along_y, along_x])


def local(images):
    own_rimmed = padded_2(images, (("slab", 1),), 4)
    next_rimmed = passed_along(own_rimmed, "phase", -1)
    own_zero = phase_stats(own_rimmed[0])
    own_one = phase_stats(own_rimmed[1])
    next_zero = phase_stats(next_rimmed[0])
    next_one = phase_stats(next_rimmed[1])
    zero_one = pair_terms(own_zero, own_one)
    one_next = pair_terms(own_one, next_zero)
    zero_next = pair_terms(own_zero, next_zero)
    one_after = pair_terms(own_one, next_one)
    coef_zero = zero_one[0] + zero_next[0]
    coef_one = zero_one[1] + one_next[0] + one_after[0]
    outgoing = jnp.stack([one_next[1] + zero_next[1], one_after[1]])
    incoming = passed_along(outgoing, "phase", 1)
    coefs = jnp.stack([coef_zero, coef_one]) + incoming
    forces = jnp.stack(
        [gradient(own_rimmed[0]) * coefs[0][None], gradient(own_rimmed[1]) * coefs[1][None]], axis=1
    )
    return forces


def solution(mesh):
    in_specs = (P("phase", "slab", None, None),)
    out_specs = P(None, "phase", "slab", None, None)
    return jax.shard_map(local, mesh=mesh, in_specs=in_specs, out_specs=out_specs, check_vma=False)
```

profile of v0, /device:TPU:225, one launch (start us, length us, event | category | flops | bytes accessed | tf_op | source)
XLA Modules:
  0.0 224.9 jit_solution(5995736477840909657)
XLA Ops:
  1.1 1.9 collective-permute-start.1
  3.0 2.6 %collective-permute-start = (f32[2,4,64,128]{3,2,1,0:T(8,128)S(1)}, f32[2,4,64,128]{3,2,1,0:T(8,128)S(1)}, u32[]{:S(2)}, u32[]{:S(2)}) collective-permute-start(f32[2,4,64,128]{3,2,1,0:T(8,128)S(1)} %get-tuple-element.44), channel_id=1, source_target_pairs={{1,0},{2,1},{3,2},{4,3},{5,4},{6,5},{7,6},{8,7},{9,8},{10,9},{11,1... | collective-permute-start | bytes 786440 | tf_op jit(solution)/shard_map/ppermute | solution.py:17
  6.3 2.3 %constant_dynamic-update-slice_fusion.5 = (f32[2,40,64,128]{3,2,1,0:T(8,128)S(1)}, f32[2,36,64,128]{3,2,1,0:T(8,128)S(1)}, f32[2,36,64,128]{3,2,1,0:T(8,128)S(1)}) fusion(f32[2,40,64,128]{3,2,1,0:T(8,128)S(1)} %get-tuple-element.51, f32[2,32,64,128]{3,2,1,0:T(8,128)} %param.1, f32[2,36,64,128]{3,2,1,0:T(8,128)S(1)} %get-tuple-element.52), kind=kLoop, calls=%fused_computation.582 | loop fusion | bytes 8388608
  8.7 4.1 %collective-permute-done = f32[2,4,64,128]{3,2,1,0:T(8,128)S(1)} collective-permute-done((f32[2,4,64,128]{3,2,1,0:T(8,128)S(1)}, f32[2,4,64,128]{3,2,1,0:T(8,128)S(1)}, u32[]{:S(2)}, u32[]{:S(2)}) %collective-permute-start) | collective-permute-done | bytes 262176 | tf_op jit(solution)/shard_map/ppermute | solution.py:17
  12.8 5.4 %collective-permute-start.2 = (f32[2,40,64,128]{3,2,1,0:T(8,128)S(1)}, f32[2,40,64,128]{3,2,1,0:T(8,128)S(1)}, u32[]{:S(2)}, u32[]{:S(2)}) collective-permute-start(f32[2,40,64,128]{3,2,1,0:T(8,128)S(1)} %get-tuple-element.49), channel_id=1, source_target_pairs={{0,224},{32,0},{64,32},{96,64},{128,96},{160,128},{192,160},{224,1... | collective-permute-start | bytes 7864328 | tf_op jit(solution)/shard_map/ppermute | solution.py:25
  18.2 2.2 fusion.243
  20.5 2.7 %fusion.15 = (f32[32,64,128]{2,1,0:T(8,128)}, f32[32,64,128]{2,1,0:T(8,128)}) fusion(f32[32,64,128]{2,1,0:T(8,128)S(1)} %get-tuple-element.21, f32[32,64,128]{2,1,0:T(8,128)S(1)} %get-tuple-element.20), kind=kLoop, calls=%fused_computation.228 | loop fusion | flops 4194304 | bytes 4194304 | tf_op jit(solution)/shard_map/add | solution.py:35
  23.2 51.2 %collective-permute-done.2 = f32[2,40,64,128]{3,2,1,0:T(8,128)S(1)} collective-permute-done((f32[2,40,64,128]{3,2,1,0:T(8,128)S(1)}, f32[2,40,64,128]{3,2,1,0:T(8,128)S(1)}, u32[]{:S(2)}, u32[]{:S(2)}) %collective-permute-start.2) | collective-permute-done | bytes 2621472 | tf_op jit(solution)/shard_map/ppermute | solution.py:25
  74.3 1.9 slice_multiply_fusion.1
  76.2 2.4 %fusion.240 = (f32[32,64,128]{2,1,0:T(8,128)S(1)}, f32[32,64,128]{2,1,0:T(8,128)S(1)}) fusion(f32[1,40,64,128]{3,2,1,0:T(8,128)S(1)} %get-tuple-element.24, f32[1,40,64,128]{3,2,1,0:T(8,128)S(1)} %get-tuple-element.32), kind=kLoop, calls=%fused_computation.504 | loop fusion | flops 4194304 | bytes 20971520 | tf_op jit(solution)/shard_map/add | solution.py:30
  80.3 2.2 fusion.232
  84.3 2.2 fusion.242
  86.5 1.8 fusion.31
  90.0 2.4 %fusion.224 = (f32[32,64,128]{2,1,0:T(8,128)S(1)}, f32[32,64,128]{2,1,0:T(8,128)S(1)}) fusion(f32[1,40,64,128]{3,2,1,0:T(8,128)S(1)} %get-tuple-element.35, f32[1,40,64,128]{3,2,1,0:T(8,128)S(1)} %get-tuple-element.22), kind=kLoop, calls=%fused_computation.440 | loop fusion | flops 4194304 | bytes 20971520 | tf_op jit(solution)/shard_map/add | solution.py:30
  94.2 1.8 fusion.95
  96.0 1.8 fusion.71
  97.8 2.2 fusion.225
  100.0 2.7 %fusion.55 = (f32[32,64,128]{2,1,0:T(8,128)}, f32[32,64,128]{2,1,0:T(8,128)}) fusion(f32[32,64,128]{2,1,0:T(8,128)S(1)} %get-tuple-element.30, f32[32,64,128]{2,1,0:T(8,128)S(1)} %get-tuple-element.29), kind=kLoop, calls=%fused_computation.268 | loop fusion | flops 4194304 | bytes 4194304 | tf_op jit(solution)/shard_map/add | solution.py:35
  102.7 32.7 %add_bitcast_fusion.2 = (f32[1,32,64,128]{3,2,1,0:T(8,128)}, f32[32,64,128]{2,1,0:T(8,128)}, f32[32,64,128]{2,1,0:T(8,128)}, f32[32,64,128]{2,1,0:T(8,128)}, f32...) fusion(f32[2,32,64,128]{3,2,1,0:T(8,128)S(1)} %copy-done.2, ...), kind=kLoop, calls=%fused_computation.569 | loop fusion | flops 27000832 | bytes 22020096 | tf_op jit(solution)/shard_map/stack | solution.py:86
  135.4 27.4 %add_bitcast_fusion.1 = (f32[1,32,64,128]{3,2,1,0:T(8,128)}, f32[32,64,128]{2,1,0:T(8,128)}, f32[32,64,128]{2,1,0:T(8,128)}, f32[32,64,128]{2,1,0:T(8,128)}, f32[32,64,128]{2,1,0:T(8,128)}) fusion(f32[32,64,128]{2,1,0:T(8,128)} %get-tuple-element.13, f32[32,64,128]{2,1,0:T(8,128)} %get-tuple-element.6, f32[32,64,128]{2,1,0:T(8,128)} %get-tuple-element.12, ...), kind=kLoop, calls=%fused_computation.566 | loop fusion | flops 18874368 | bytes 20971520 | tf_op jit(solution)/shard_map/stack | solution.py:86
  162.8 5.5 %add_bitcast_fusion = (f32[1,32,64,128]{3,2,1,0:T(8,128)S(1)}, f32[1,32,64,128]{3,2,1,0:T(8,128)S(1)}) fusion(f32[32,64,128]{2,1,0:T(8,128)} %get-tuple-element.9, f32[32,64,128]{2,1,0:T(8,128)} %get-tuple-element.13, f32[32,64,128]{2,1,0:T(8,128)} %get-tuple-element.16, f32[32,64,128]{2,1,0:T(8,128)} %get-tuple-element.8, ...), kind=kLoop, calls=%fused_computation.565 | loop fusion | flops 7864320 | bytes 16777216 | tf_op jit(solution)/shard_map/stack | solution.py:84
  168.6 1.9 collective-permute-start.3
  173.5 46.6 %collective-permute-done.3 = f32[2,32,64,128]{3,2,1,0:T(8,128)S(1)} collective-permute-done((f32[2,32,64,128]{3,2,1,0:T(8,128)S(1)}, f32[2,32,64,128]{3,2,1,0:T(8,128)S(1)}, u32[]{:S(2)}, u32[]{:S(2)}) %collective-permute-start.3) | collective-permute-done | bytes 2097184 | tf_op jit(solution)/shard_map/ppermute | solution.py:25
  221.6 3.3 %pad_maximum_fusion = f32[3,2,32,64,128]{4,3,2,1,0:T(8,128)} fusion(f32[3,1,32,64,128]{4,3,2,1,0:T(8,128)S(1)} %maximum_multiply_fusion.1, f32[3,1,32,64,128]{4,3,2,1,0:T(8,128)S(1)} %maximum_multiply_fusion), kind=kLoop, calls=%fused_computation | loop fusion | flops 1572864 | bytes 12582912 | tf_op jit(solution)/shard_map/stack | solution.py:87
  (35 shorter events, 13.5 us)
Async XLA Ops:
  1.1 5.2 %collective-permute-start.1 = (f32[2,4,64,128]{3,2,1,0:T(8,128)S(1)}, f32[2,4,64,128]{3,2,1,0:T(8,128)S(1)}, u32[]{:S(2)}, u32[]{:S(2)}) collective-permute-start(f32[2,4,64,128]{3,2,1,0:T(8,128)S(1)} %get-tuple-element.43), channel_id=1, source_target_pairs={{0,1},{1,2},{2,3},{3,4},{4,5},{5,6},{6,7},{7,8},{8,9},{9,10},{10,1... | collective-permute-start | bytes 786440 | tf_op jit(solution)/shard_map/ppermute | solution.py:16
  3.0 9.8 %collective-permute-start = (f32[2,4,64,128]{3,2,1,0:T(8,128)S(1)}, f32[2,4,64,128]{3,2,1,0:T(8,128)S(1)}, u32[]{:S(2)}, u32[]{:S(2)}) collective-permute-start(f32[2,4,64,128]{3,2,1,0:T(8,128)S(1)} %get-tuple-element.44), channel_id=1, source_target_pairs={{1,0},{2,1},{3,2},{4,3},{5,4},{6,5},{7,6},{8,7},{9,8},{10,9},{11,1... | collective-permute-start | bytes 786440 | tf_op jit(solution)/shard_map/ppermute | solution.py:17
  6.3 11.9 %copy-start.2 = (f32[2,32,64,128]{3,2,1,0:T(8,128)S(1)}, f32[2,32,64,128]{3,2,1,0:T(8,128)}, u32[]{:S(2)}) copy-start(f32[2,32,64,128]{3,2,1,0:T(8,128)} %param.1) | copy-start | bytes 6291460
  8.7 11.7 %copy-start.4 = (f32[2,36,64,128]{3,2,1,0:T(8,128)}, f32[2,36,64,128]{3,2,1,0:T(8,128)S(1)}, u32[]{:S(2)}) copy-start(f32[2,36,64,128]{3,2,1,0:T(8,128)S(1)} %get-tuple-element.41) | copy-start | bytes 7077892
  12.8 7.6 %copy-start = (f32[2,36,64,128]{3,2,1,0:T(8,128)}, f32[2,36,64,128]{3,2,1,0:T(8,128)S(1)}, u32[]{:S(2)}) copy-start(f32[2,36,64,128]{3,2,1,0:T(8,128)S(1)} %get-tuple-element.50) | copy-start | bytes 7077892
  12.8 61.5 %collective-permute-start.2 = (f32[2,40,64,128]{3,2,1,0:T(8,128)S(1)}, f32[2,40,64,128]{3,2,1,0:T(8,128)S(1)}, u32[]{:S(2)}, u32[]{:S(2)}) collective-permute-start(f32[2,40,64,128]{3,2,1,0:T(8,128)S(1)} %get-tuple-element.49), channel_id=1, source_target_pairs={{0,224},{32,0},{64,32},{96,64},{128,96},{160,128},{192,160},{224,1... | collective-permute-start | bytes 7864328 | tf_op jit(solution)/shard_map/ppermute | solution.py:25
  100.0 2.7 %copy-start.7 = (f32[32,64,128]{2,1,0:T(8,128)S(1)}, f32[32,64,128]{2,1,0:T(8,128)}, u32[]{:S(2)}) copy-start(f32[32,64,128]{2,1,0:T(8,128)} %fusion.63) | copy-start | bytes 3145732
  168.3 2.2 copy-start.3
  168.6 51.5 %collective-permute-start.3 = (f32[2,32,64,128]{3,2,1,0:T(8,128)S(1)}, f32[2,32,64,128]{3,2,1,0:T(8,128)S(1)}, u32[]{:S(2)}, u32[]{:S(2)}) collective-permute-start(f32[2,32,64,128]{3,2,1,0:T(8,128)S(1)} %pad_maximum_fusion.1), channel_id=1, source_target_pairs={{0,32},{32,64},{64,96},{96,128},{128,160},{160,192},{192,224},{224... | collective-permute-start | bytes 6291464 | tf_op jit(solution)/shard_map/ppermute | solution.py:25
  170.7 1.8 copy-start.1
  170.7 2.4 %copy-start.5 = (f32[2,36,64,128]{3,2,1,0:T(8,128)S(1)}, f32[2,36,64,128]{3,2,1,0:T(8,128)}, u32[]{:S(2)}) copy-start(f32[2,36,64,128]{3,2,1,0:T(8,128)} %copy-done.4) | copy-start | bytes 7077892
  173.1 47.1 %copy-start.6 = (f32[1,32,64,128]{3,2,1,0:T(8,128)S(1)}, f32[1,32,64,128]{3,2,1,0:T(8,128)}, u32[]{:S(2)}) copy-start(f32[1,32,64,128]{3,2,1,0:T(8,128)} %get-tuple-element.15) | copy-start | bytes 3145732
  173.1 47.1 %copy-start.8 = (f32[1,32,64,128]{3,2,1,0:T(8,128)S(1)}, f32[1,32,64,128]{3,2,1,0:T(8,128)}, u32[]{:S(2)}) copy-start(f32[1,32,64,128]{3,2,1,0:T(8,128)} %get-tuple-element.5) | copy-start | bytes 3145732
where the time goes:
time: 225 us
  other arithmetic  106 us (47%)
  waiting for transfers between devices  103 us (46%)
  starting transfers between devices  11.8 us (5%)
  local copies, waits for them, and re-layouts  4.36 us (2%)
    ppermute x2, waiting for transfers between devices, passed_along(): return lax.ppermute(value, axis, pairs)  97.8 us
    another operation x2, other arithmetic, local(): coefs = jnp.stack([coef_zero, coef_one]) + incoming  60.1 us
    add x10, other arithmetic, window_mean(): sum((lax.slice_in_dim(padded, offset, offset + length, axis=direction) fo...  17.8 us
    add x6, other arithmetic, window_mean(): summed = sum((field[offset:offset + inner_depth] for offset in range(9)))  13.5 us
    ppermute x2, starting transfers between devices, passed_along(): return lax.ppermute(value, axis, pairs)  7.31 us
    another operation x2, other arithmetic, local(): outgoing = jnp.stack([one_next[1] + zero_next[1], one_after[1]])  5.74 us
  transfers between devices with their start and end apart: 4, of which 4 were waited for; matrix products, arithmetic and copies ran while one was open for 4% of the time, Pallas kernels for 0%

commit v1 on v0

v1 whole, which is shorter than its diff:
```python
import functools

import jax
import jax.numpy as jnp
from jax import lax
from jax.experimental import pallas as pl
from jax.experimental.pallas import tpu as pltpu
from jax.sharding import PartitionSpec as P

EPSILON = 1e-05
MESH = pl.DeviceIdType.MESH
PAIRS = ((2, 3), (2, 4), (2, 1), (2, 0), (3, 4), (3, 5), (3, 1))
FIELDS = 12 + len(PAIRS)
CY, CX = 64, 128
DEPTH = 32
BLOCK = 4


def plane_windows(at, buf, padded, partial, operand, band, windows):
    values = [buf[j, at] for j in range(6)]
    for f in range(FIELDS):
        if f < 6:
            field = values[f]
        elif f < 12:
            field = values[f - 6] * values[f - 6]
        else:
            a, b = PAIRS[f - 12]
            field = values[a] * values[b]
        padded[f, 8:72, :] = field
    for f in range(FIELDS):
        partial[f] = padded[f, 3:75, :] + padded[f, 4:76, :] + padded[f, 5:77, :]
    for f in range(FIELDS):
        summed = partial[f, 1:65, :] + partial[f, 4:68, :] + partial[f, 7:71, :]
        high = summed.astype(jnp.bfloat16)
        rest = summed - high.astype(jnp.float32)
        middle = rest.astype(jnp.bfloat16)
        low = (rest - middle.astype(jnp.float32)).astype(jnp.bfloat16)
        rows = slice(f * CY, (f + 1) * CY)
        operand[rows, 0:128] = high
        operand[rows, 128:256] = middle
        operand[rows, 256:384] = low
    windows[at] = jnp.dot(operand[...], band[...], preferred_element_type=jnp.float32)


def block_coefs(c, buf, windows, coef_ref):
    first = c * BLOCK

    @pl.loop(0, CY // 8)
    def _(r):
        sums = []
        for f in range(FIELDS):
            rows = pl.ds(pl.multiple_of(f * CY + r * 8, 8), 8)
            p = [windows[first + i, rows, :] for i in range(12)]
            common = (p[3] + p[4]) + (p[5] + p[6]) + (p[7] + p[8])
            left = p[1] + p[2]
            right = p[9] + p[10]
            sums.append(
                [common + (p[0] + left), common + (left + p[9]), common + (p[2] + right), common + (right + p[11])]
            )
        tile = pl.ds(pl.multiple_of(r * 8, 8), 8)
        for i in range(BLOCK):
            total = [s[i] * (1.0 / 729.0) for s in sums]
            mean = total[:6]
            spread = [total[6 + j] - mean[j] * mean[j] for j in range(6)]
            offset = [buf[j, first + 4 + i, tile, :] - mean[j] for j in range(6)]
            along = {2: 0.0, 3: 0.0}
            across = {2: 0.0, 3: 0.0}
            for k, (a, b) in enumerate(PAIRS):
                covariance = total[12 + k] - mean[a] * mean[b]
                weight = 2.0 * covariance / (spread[a] * spread[b] + EPSILON)
                scaled = weight * covariance
                along[a] += weight * offset[b]
                across[a] += scaled
                if b == 3:
                    along[b] += weight * offset[a]
                    across[b] += scaled
            for own in (2, 3):
                coef_ref[own - 2, first + i, tile, :] = (
                    along[own] - across[own] / (spread[own] + EPSILON) * offset[own]
                )


def coef_kernel(
    images, coef_ref, rim_ref, buf, padded, partial, operand, band, windows,
    x_send, x_recv, y_send, y_recv, rim_send, rim_recv, local_sem,
):
    phase, slab = lax.axis_index("phase"), lax.axis_index("slab")
    slabs = lax.axis_size("slab")
    y, side = phase // 2, phase % 2
    partner = (y * 2 + 1 - side, slab)
    y_to = ((y + 1 + 2 * side) % 4 * 2 + side, slab)
    y_from = ((y + 3 + 2 * side) % 4 * 2 + side, slab)
    below = (phase, (slab + slabs - 1) % slabs)
    above = (phase, (slab + 1) % slabs)

    barrier = pltpu.get_barrier_semaphore()
    for peer in (partner, y_to, y_from, below, above):
        pl.semaphore_signal(barrier, inc=1, device_id=peer, device_id_type=MESH)
    pl.semaphore_wait(barrier, 5)

    from_x, from_y = 4 - 4 * side, 4 * side

    def plane_of(k):
        return (k + DEPTH - 4) % DEPTH

    def x_copy(k, slot):
        z = plane_of(k)
        return pltpu.make_async_remote_copy(
            images.at[:, pl.ds(z, 1)], buf.at[pl.ds(slot, 2), pl.ds(4 + z, 1)],
            x_send.at[k], x_recv.at[k], device_id=partner, device_id_type=MESH,
        )

    def y_copy(k):
        z = plane_of(k)
        return pltpu.make_async_remote_copy(
            buf.at[pl.ds(from_x, 2), pl.ds(4 + z, 1)], buf.at[pl.ds(from_y, 2), pl.ds(4 + z, 1)],
            y_send.at[k], y_recv.at[k], device_id=y_to, device_id_type=MESH,
        )

    def rim_copy(which, up):
        slot = (2, from_x, from_y)[which]
        source = pl.ds(DEPTH, 4) if up else pl.ds(4, 4)
        target = pl.ds(0, 4) if up else pl.ds(DEPTH + 4, 4)
        return pltpu.make_async_remote_copy(
            buf.at[pl.ds(slot, 2), source], buf.at[pl.ds(slot, 2), target],
            rim_send.at[which, up], rim_recv.at[which, up],
            device_id=above if up else below, device_id_type=MESH,
        )

    def each_rim(whiches, ups, act, arriving):
        for up in ups:
            edge = (0 if arriving else slabs - 1) if up else (slabs - 1 if arriving else 0)

            @pl.when(slab != edge)
            def _():
                for which in whiches:
                    act(rim_copy(which, up))

    @pl.loop(0, DEPTH)
    def _(k):
        x_copy(k, from_y).start()

    own = pltpu.make_async_copy(images, buf.at[pl.ds(2, 2), pl.ds(4, DEPTH)], local_sem)
    own.start()

    @pl.when(slab == 0)
    def _():
        buf[:, 0:4] = jnp.zeros((6, 4, CY, CX), jnp.float32)

    @pl.when(slab == slabs - 1)
    def _():
        buf[:, DEPTH + 4 : DEPTH + 8] = jnp.zeros((6, 4, CY, CX), jnp.float32)

    padded[:, 0:8, :] = jnp.zeros((FIELDS, 8, CX), jnp.float32)
    padded[:, 72:80, :] = jnp.zeros((FIELDS, 8, CX), jnp.float32)
    row = lax.broadcasted_iota(jnp.int32, (128, 128), 0)
    column = lax.broadcasted_iota(jnp.int32, (128, 128), 1)
    near = jnp.where(jnp.abs(row - column) <= 4, 1.0, 0.0).astype(jnp.bfloat16)
    for i in range(3):
        band[i * 128 : (i + 1) * 128, :] = near
    own.wait()
    each_rim((0,), (0, 1), lambda copy: copy.start(), False)

    def serve(k):
        x_copy(k, from_x).wait_recv()
        y_copy(k).start()

    serve(0)

    @pl.loop(0, DEPTH)
    def _(u):
        @pl.when(u < DEPTH - 1)
        def _():
            serve(u + 1)

        y_copy(u).wait_recv()

        @pl.when(u == 3)
        def _():
            each_rim((1, 2), (1,), lambda copy: copy.start(), False)

        @pl.when(u == 7)
        def _():
            each_rim((1, 2), (0,), lambda copy: copy.start(), False)

        @pl.when(u == 16)
        def _():
            each_rim((0, 1, 2), (0, 1), lambda copy: copy.wait_recv(), True)

        eighth = u // 8
        twice = eighth // 2 * (1 - eighth % 2)

        @pl.loop(0, 1 + twice)
        def _(w):
            r = (u - 16) * w
            at = (1 - w) * (plane_of(u) + 4) + w * (r + DEPTH * (r // 4))
            plane_windows(at, buf, padded, partial, operand, band, windows)

        @pl.when((u >= 24) & (u < 29))
        def _():
            block_coefs(u - 24, buf, windows, coef_ref)

    @pl.loop(5, DEPTH // BLOCK)
    def _(c):
        block_coefs(c, buf, windows, coef_ref)

    rim_ref[:, 0] = buf[2:4, 3]
    rim_ref[:, 1] = buf[2:4, DEPTH + 4]

    @pl.loop(0, DEPTH)
    def _(k):
        x_copy(k, from_y).wait_send()
        y_copy(k).wait_send()

    each_rim((0, 1, 2), (0, 1), lambda copy: copy.wait_send(), False)


def force_kernel(depth, coef_ref, image_ref, below_ref, above_ref, rim_ref, out_ref):
    j, last = pl.program_id(1), pl.num_programs(1) - 1
    below = jnp.where(j == 0, rim_ref[0, 0], below_ref[0, 0])
    above = jnp.where(j == last, rim_ref[0, 1], above_ref[0, 0])
    row = lax.broadcasted_iota(jnp.int32, (CY, CX), 0)
    column = lax.broadcasted_iota(jnp.int32, (CY, CX), 1)
    for i in range(depth):
        half = coef_ref[0, i] * 0.5
        here = image_ref[0, i]
        up = image_ref[0, i + 1] if i + 1 < depth else above
        down = image_ref[0, i - 1] if i else below
        out_ref[0, 0, i] = half * (up - down)
        up = jnp.where(row < CY - 1, pltpu.roll(here, CY - 1, 0), 0.0)
        down = jnp.where(row > 0, pltpu.roll(here, 1, 0), 0.0)
        out_ref[1, 0, i] = half * (up - down)
        up = jnp.where(column < CX - 1, pltpu.roll(here, CX - 1, 1), 0.0)
        down = jnp.where(column > 0, pltpu.roll(here, 1, 1), 0.0)
        out_ref[2, 0, i] = half * (up - down)


def local(images):
    f32, vmem = jnp.float32, pl.BlockSpec(memory_space=pltpu.VMEM)
    dma = pltpu.SemaphoreType.DMA
    coefs, rims = pl.pallas_call(
        coef_kernel,
        out_shape=(
            jax.ShapeDtypeStruct((2, DEPTH, CY, CX), f32),
            jax.ShapeDtypeStruct((2, 2, CY, CX), f32),
        ),
        in_specs=[pl.BlockSpec(memory_space=pl.ANY)],
        out_specs=(vmem, vmem),
        scratch_shapes=[
            pltpu.VMEM((6, DEPTH + 8, CY, CX), f32),
            pltpu.VMEM((FIELDS, 80, CX), f32),
            pltpu.VMEM((FIELDS, 72, CX), f32),
            pltpu.VMEM((FIELDS * CY, 384), jnp.bfloat16),
            pltpu.VMEM((384, CX), jnp.bfloat16),
            pltpu.VMEM((DEPTH + 8, FIELDS * CY, CX), f32),
            dma((DEPTH,)), dma((DEPTH,)), dma((DEPTH,)), dma((DEPTH,)),
            dma((3, 2)), dma((3, 2)), dma,
        ],
        compiler_params=pltpu.CompilerParams(
            collective_id=0, has_side_effects=True, vmem_limit_bytes=56 * 2**20
        ),
        name="coefs",
    )(images)
    depth = 8
    block = (1, depth, CY, CX)
    plane = (1, 1, CY, CX)
    return pl.pallas_call(
        functools.partial(force_kernel, depth),
        out_shape=jax.ShapeDtypeStruct((3, 2, DEPTH, CY, CX), f32),
        grid=(2, DEPTH // depth),
        in_specs=[
            pl.BlockSpec(block, lambda p, j: (p, j, 0, 0)),
            pl.BlockSpec(block, lambda p, j: (p, j, 0, 0)),
            pl.BlockSpec(plane, lambda p, j: (p, jnp.maximum(j * depth - 1, 0), 0, 0)),
            pl.BlockSpec(plane, lambda p, j: (p, jnp.minimum(j * depth + depth, DEPTH - 1), 0, 0)),
            pl.BlockSpec((1, 2, CY, CX), lambda p, j: (p, 0, 0, 0)),
        ],
        out_specs=pl.BlockSpec((3, 1, depth, CY, CX), lambda p, j: (0, p, j, 0, 0)),
        name="forces",
    )(coefs, images, images, images, rims)


def solution(mesh):
    in_specs = (P("phase", "slab", None, None),)
    out_specs = P(None, "phase", "slab", None, None)
    return jax.shard_map(local, mesh=mesh, in_specs=in_specs, out_specs=out_specs, check_vma=False)
```

time: 225 us -> 109 us (0.48)
  the two profiles are of different devices: /device:TPU:225 before, /device:TPU:16 now
where the time goes in v1:
time: 109 us; the launch traced here: 108 us
  Pallas kernels  108 us (99%)
    pallas_call x1, Pallas kernels, local(): pl.pallas_call(coef_kernel, out_shape=(jax.ShapeDtypeStruct((2, DEPTH, CY...  99.7 us
    pallas_call x1, Pallas kernels, local(): pl.pallas_call(functools.partial(force_kernel, depth), out_shape=jax.Shap...  7.85 us

profile of v1, /device:TPU:16, one launch (start us, length us, event | category | flops | bytes accessed | tf_op | source)
XLA Modules:
  0.0 107.6 jit_solution(6212868713923832409)
XLA Ops:
  0.0 99.7 %coefs.1 = (f32[2,32,64,128]{3,2,1,0:T(8,128)}, f32[2,2,64,128]{3,2,1,0:T(8,128)}) custom-call(f32[2,32,64,128]{3,2,1,0:T(8,128)} %above_ref.1), custom_call_target="tpu_custom_call" | custom-call | tf_op jit(solution)/shard_map/coefs/pallas_call | solution.py:241
  99.7 7.9 %forces.1 = f32[3,2,32,64,128]{4,3,2,1,0:T(8,128)} custom-call(f32[2,32,64,128]{3,2,1,0:T(8,128)} %get-tuple-element.7.coef_ref, f32[2,32,64,128]{3,2,1,0:T(8,128)} %above_ref.1, f32[2,32,64,128]{3,2,1,0:T(8,128)} %above_ref.1, f32[2,32,64,128]{3,2,1,0:T(8,128)} %above_ref.1, f32[2,2,64,128]{3,2,1,0:T(8,128)} %get-tuple-element.8.rim_ref), custom_call_target="tpu_custom_call" | custom-call | tf_op jit(solution)/shard_map/forces/pallas_call | solution.py:267

commit v2 on v1

v2 whole, which is shorter than its diff:
```python
import jax
import jax.numpy as jnp
from jax import lax
from jax.experimental import pallas as pl
from jax.experimental.pallas import tpu as pltpu
from jax.sharding import PartitionSpec as P

EPSILON = 1e-05
MESH = pl.DeviceIdType.MESH
SOON = (0, 1, 2, 3, (0, 0), (1, 1), (2, 2), (3, 3), (0, 1), (0, 2), (1, 2), (1, 3))
LATE = (4, 5, (4, 4), (5, 5), (0, 5), (0, 4), (1, 5))
ORDER = SOON + LATE
PAIRS = tuple(f for f in ORDER if f not in range(6) and f[0] != f[1])
FIELDS = len(ORDER)
CY, CX = 64, 128
DEPTH = 32
SENT = {(1, 1): 0, (2, 1): 3, (1, 0): 4, (2, 0): 7}
RELAY = 6
BLOCKS = ((0, 7, 20), (7, 8, 24), (15, 4, 27), (19, 4, 30))
LAST = 23
STORE = 4
LAG = 4


def plane_windows(fields, at, place, buf, padded, partial, operand, band, windows):
    base, count = ORDER.index(fields[0]), len(fields)
    images = {j: buf[place[j], at] for j in range(6) if any(j == f or f not in range(6) and j in f for f in fields)}
    for f, field in enumerate(fields, base):
        padded[f, 8:72, :] = images[field] if field in range(6) else images[field[0]] * images[field[1]]
    for f in range(base, base + count):
        partial[f] = padded[f, 3:75, :] + padded[f, 4:76, :] + padded[f, 5:77, :]
    for f in range(base, base + count):
        summed = partial[f, 1:65, :] + partial[f, 4:68, :] + partial[f, 7:71, :]
        high = summed.astype(jnp.bfloat16)
        rest = summed - high.astype(jnp.float32)
        middle = rest.astype(jnp.bfloat16)
        low = (rest - middle.astype(jnp.float32)).astype(jnp.bfloat16)
        rows = slice(f * CY, (f + 1) * CY)
        operand[rows, 0:128] = high
        operand[rows, 128:256] = middle
        operand[rows, 256:384] = low
    rows = slice(base * CY, (base + count) * CY)
    windows[at, rows] = jnp.dot(operand[rows, :], band[...], preferred_element_type=jnp.float32)


def block_coefs(first, size, place, buf, windows, coef_ref):
    @pl.loop(0, CY // 8)
    def _(r):
        sums = []
        for f in range(FIELDS):
            p = windows[pl.ds(first, size + 8), pl.ds(pl.multiple_of(f * CY + r * 8, 8), 8), :]
            common = p[size - 1]
            for i in range(size, 9):
                common = common + p[i]
            left, right = {}, {}
            for i in reversed(range(size - 1)):
                left[i] = p[i] + left[i + 1] if i + 1 in left else p[i]
            for i in range(1, size):
                right[i] = right[i - 1] + p[8 + i] if i - 1 in right else p[8 + i]
            sums.append([])
            for i in range(size):
                ends = [part[i] for part in (left, right) if i in part]
                sums[f].append(common + (ends[0] + ends[1] if len(ends) == 2 else ends[0]))
        tile = pl.ds(pl.multiple_of(r * 8, 8), 8)
        for i in range(size):
            total = {field: s[i] * (1.0 / 729.0) for field, s in zip(ORDER, sums)}
            spread = [total[j, j] - total[j] * total[j] for j in range(6)]
            offset = [buf[place[j], first + 4 + i, tile, :] - total[j] for j in range(6)]
            along, across = [0.0, 0.0], [0.0, 0.0]
            for a, b in PAIRS:
                covariance = total[a, b] - total[a] * total[b]
                weight = 2.0 * covariance / (spread[a] * spread[b] + EPSILON)
                scaled = weight * covariance
                for own, other in ((a, b), (b, a)):
                    if own < 2:
                        along[own] += weight * offset[other]
                        across[own] += scaled
            for own in (0, 1):
                coef_ref[place[own] - 2, first + i, tile, :] = (
                    along[own] - across[own] / (spread[own] + EPSILON) * offset[own]
                )


def coef_kernel(
    images, coef_ref, gradient_ref, buf, padded, partial, operand, band, windows,
    x_send, x_recv, y_send, y_recv, rim_send, rim_recv, relay_send, relay_recv, local_sem, relay,
):
    phase, slab = lax.axis_index("phase"), lax.axis_index("slab")
    slabs = lax.axis_size("slab")
    y, side = phase // 2, phase % 2
    partner = (y * 2 + 1 - side, slab)
    y_to = ((y + 1 + 2 * side) % 4 * 2 + side, slab)
    y_from = ((y + 3 + 2 * side) % 4 * 2 + side, slab)
    below = (phase, (slab + slabs - 1) % slabs)
    above = (phase, (slab + 1) % slabs)

    barrier = pltpu.get_barrier_semaphore()
    for peer in (partner, y_to, y_from, below, above):
        pl.semaphore_signal(barrier, inc=1, device_id=peer, device_id_type=MESH)

    middle = slabs // 2
    relays = {(1, 1): middle + 2, (2, 1): slabs - 4, (1, 0): middle - 3, (2, 0): 3}
    ends = (slab == middle - 1) | (slab == middle)
    passes = (slab == middle + 2) | (slab == slabs - 4) | (slab == middle - 3) | (slab == 3)

    @pl.when(ends)
    def _():
        for peer in relays.values():
            pl.semaphore_signal(barrier, inc=1, device_id=(phase, peer), device_id_type=MESH)
        pl.semaphore_wait(barrier, 9)

    @pl.when(passes)
    def _():
        for peer in (middle - 1, middle):
            pl.semaphore_signal(barrier, inc=1, device_id=(phase, peer), device_id_type=MESH)
        pl.semaphore_wait(barrier, 7)

    @pl.when(jnp.logical_not(ends | passes))
    def _():
        pl.semaphore_wait(barrier, 5)

    from_x, from_y = 4 - 4 * side, 4 * side
    place = (2 + side, 3 - side, from_x + side, from_x + 1 - side, from_y + side, from_y + 1 - side)

    def plane_of(k):
        return (k + DEPTH - 4) % DEPTH

    def x_copy(k, slot):
        z = plane_of(k)
        return pltpu.make_async_remote_copy(
            images.at[:, pl.ds(z, 1)], buf.at[pl.ds(slot, 2), pl.ds(4 + z, 1)],
            x_send.at[k], x_recv.at[k], device_id=partner, device_id_type=MESH,
        )

    def y_copy(k):
        z = plane_of(k)
        return pltpu.make_async_remote_copy(
            buf.at[pl.ds(from_x, 2), pl.ds(4 + z, 1)], buf.at[pl.ds(from_y, 2), pl.ds(4 + z, 1)],
            y_send.at[k], y_recv.at[k], device_id=y_to, device_id_type=MESH,
        )

    def rim_copy(which, up):
        slot = (2, from_x, from_y)[which]
        source = pl.ds(DEPTH, 4) if up else pl.ds(4, 4)
        target = pl.ds(0, 4) if up else pl.ds(DEPTH + 4, 4)
        return pltpu.make_async_remote_copy(
            buf.at[pl.ds(slot, 2), source], buf.at[pl.ds(slot, 2), target],
            rim_send.at[which, up], rim_recv.at[which, up],
            device_id=above if up else below, device_id_type=MESH,
        )

    def to_relay(which, up):
        slot = (2, from_x, from_y)[which]
        return pltpu.make_async_remote_copy(
            buf.at[pl.ds(slot, 2), pl.ds(DEPTH, 4) if up else pl.ds(4, 4)], relay,
            relay_send.at[which], relay_recv, device_id=(phase, relays[which, up]), device_id_type=MESH,
        )

    def from_relay(which, up):
        slot = (2, from_x, from_y)[which]
        return pltpu.make_async_remote_copy(
            relay, buf.at[pl.ds(slot, 2), pl.ds(0, 4) if up else pl.ds(DEPTH + 4, 4)],
            relay_send.at[0], rim_recv.at[which, up],
            device_id=(phase, middle if up else middle - 1), device_id_type=MESH,
        )

    def send_rims(whiches, up, act):
        edge, end = (slabs - 1, middle - 1) if up else (0, middle)

        @pl.when((slab != edge) & (slab != end))
        def _():
            for which in whiches:
                act(rim_copy(which, up))

        @pl.when(slab == end)
        def _():
            for which in whiches:
                act(to_relay(which, up) if which else rim_copy(which, up))

    def await_rims(whiches, up):
        @pl.when(slab != (0 if up else slabs - 1))
        def _():
            for which in whiches:
                rim_copy(which, up).wait_recv()

    @pl.loop(0, DEPTH)
    def _(k):
        x_copy(k, from_y).start()

    own = pltpu.make_async_copy(images, buf.at[pl.ds(2, 2), pl.ds(4, DEPTH)], local_sem)
    own.start()

    @pl.when(slab == 0)
    def _():
        buf[:, 0:4] = jnp.zeros((6, 4, CY, CX), jnp.float32)

    @pl.when(slab == slabs - 1)
    def _():
        buf[:, DEPTH + 4 : DEPTH + 8] = jnp.zeros((6, 4, CY, CX), jnp.float32)

    padded[:, 0:8, :] = jnp.zeros((FIELDS, 8, CX), jnp.float32)
    padded[:, 72:80, :] = jnp.zeros((FIELDS, 8, CX), jnp.float32)
    row = lax.broadcasted_iota(jnp.int32, (128, 128), 0)
    column = lax.broadcasted_iota(jnp.int32, (128, 128), 1)
    near = jnp.where(jnp.abs(row - column) <= 4, 1.0, 0.0).astype(jnp.bfloat16)
    for i in range(3):
        band[i * 128 : (i + 1) * 128, :] = near
    own.wait()
    for up in (0, 1):
        send_rims((0,), up, lambda copy: copy.start())

    def serve(k):
        x_copy(k, from_x).wait_recv()
        y_copy(k).start()

    def work(fields, at):
        plane_windows(fields, at, place, buf, padded, partial, operand, band, windows)

    def coefs_of(first, size):
        block_coefs(first, size, place, buf, windows, coef_ref)

    @pl.loop(0, DEPTH + LAG)
    def _(t):
        u = t - LAG

        @pl.when(t < DEPTH)
        def _():
            serve(t)
            work(SOON, plane_of(t) + 4)

        @pl.when(u >= 0)
        def _():
            y_copy(u).wait_recv()
            work(LATE, plane_of(u) + 4)

        for (which, up), step in SENT.items():
            @pl.when(u == step)
            def _():
                send_rims((which,), up, lambda copy: copy.start())

        for (which, up), slab_between in relays.items():
            @pl.when((u == SENT[which, up] + RELAY) & (slab == slab_between))
            def _():
                to_relay(which, up).wait_recv()
                from_relay(which, up).start()

        @pl.when(u == 8)
        def _():
            await_rims((0,), 0)
            await_rims((0,), 1)

        @pl.when((u >= 8) & (u < 16))
        def _():
            @pl.loop(0, 4)
            def _(q):
                plane_gradient((u - 8) * 4 + q, buf, gradient_ref)

        @pl.when(u == 16)
        def _():
            await_rims((1, 2), 1)

        @pl.when(u == 20)
        def _():
            await_rims((1, 2), 0)

        @pl.when((u >= 16) & (u < 24))
        def _():
            at = u - 16 + DEPTH * ((u - 16) // 4)
            work(SOON, at)
            work(LATE, at)

        for first, size, step in BLOCKS:
            @pl.when(u == step)
            def _():
                coefs_of(first, size)

    coefs_of(LAST, DEPTH - LAST)

    @pl.loop(0, DEPTH)
    def _(k):
        x_copy(k, from_y).wait_send()
        y_copy(k).wait_send()

    for up in (0, 1):
        send_rims((0, 1, 2), up, lambda copy: copy.wait_send())
    for (which, up), slab_between in relays.items():
        @pl.when(slab == slab_between)
        def _():
            from_relay(which, up).wait_send()


def plane_gradient(z, buf, gradient_ref):
    row = lax.broadcasted_iota(jnp.int32, (CY, CX), 0)
    column = lax.broadcasted_iota(jnp.int32, (CY, CX), 1)
    for p in range(2):
        half = buf[2 + p, z + 4] * 0.5
        gradient_ref[0, p, z] = 0.5 * (buf[2 + p, z + 5] - buf[2 + p, z + 3])
        up = jnp.where(row < CY - 1, pltpu.roll(half, CY - 1, 0), 0.0)
        down = jnp.where(row > 0, pltpu.roll(half, 1, 0), 0.0)
        gradient_ref[1, p, z] = up - down
        up = jnp.where(column < CX - 1, pltpu.roll(half, CX - 1, 1), 0.0)
        down = jnp.where(column > 0, pltpu.roll(half, 1, 1), 0.0)
        gradient_ref[2, p, z] = up - down


def force_kernel(coef, gradient, out_ref, out, sem):
    def copy(c):
        planes = pl.ds(c * STORE, STORE)
        return pltpu.make_async_copy(out.at[:, :, planes], out_ref.at[:, :, planes], sem.at[c])

    @pl.loop(0, DEPTH // STORE)
    def _(c):
        @pl.loop(0, STORE)
        def _(q):
            z = c * STORE + q
            for p in range(2):
                for k in range(3):
                    out[k, p, z] = coef[p, z] * gradient[k, p, z]

        copy(c).start()

    @pl.loop(0, DEPTH // STORE)
    def _(c):
        copy(c).wait()


def local(images):
    f32, vmem = jnp.float32, pl.BlockSpec(memory_space=pltpu.VMEM)
    dma = pltpu.SemaphoreType.DMA
    coefs, gradient = pl.pallas_call(
        coef_kernel,
        out_shape=(
            pltpu.VMEM((2, DEPTH, CY, CX), f32),
            pltpu.VMEM((3, 2, DEPTH, CY, CX), f32),
        ),
        in_specs=[pl.BlockSpec(memory_space=pltpu.HBM)],
        out_specs=(vmem, vmem),
        scratch_shapes=[
            pltpu.VMEM((6, DEPTH + 8, CY, CX), f32),
            pltpu.VMEM((FIELDS, 80, CX), f32),
            pltpu.VMEM((FIELDS, 72, CX), f32),
            pltpu.VMEM((FIELDS * CY, 384), jnp.bfloat16),
            pltpu.VMEM((384, CX), jnp.bfloat16),
            pltpu.VMEM((DEPTH + 8, FIELDS * CY, CX), f32),
            dma((DEPTH,)), dma((DEPTH,)), dma((DEPTH,)), dma((DEPTH,)),
            dma((3, 2)), dma((3, 2)), dma((3,)), dma, dma,
            pltpu.VMEM((2, 4, CY, CX), f32),
        ],
        compiler_params=pltpu.CompilerParams(
            collective_id=0, has_side_effects=True, vmem_limit_bytes=54 * 2**20
        ),
        name="coefs",
    )(images)
    return pl.pallas_call(
        force_kernel,
        out_shape=jax.ShapeDtypeStruct((3, 2, DEPTH, CY, CX), f32),
        in_specs=[vmem, vmem],
        out_specs=pl.BlockSpec(memory_space=pl.ANY),
        scratch_shapes=[pltpu.VMEM((3, 2, DEPTH, CY, CX), f32), dma((DEPTH // STORE,))],
        compiler_params=pltpu.CompilerParams(vmem_limit_bytes=16 * 2**20),
        name="forces",
    )(coefs, gradient)


def solution(mesh):
    in_specs = (P("phase", "slab", None, None),)
    out_specs = P(None, "phase", "slab", None, None)
    return jax.shard_map(local, mesh=mesh, in_specs=in_specs, out_specs=out_specs, check_vma=False)
```

time: 109 us -> 75.2 us (0.69); the launches traced: 108 us -> 75.1 us
  Pallas kernels: 108 us -> 75.1 us
    pallas_call x2, Pallas kernels: 108 us -> 75.1 us  [the longest x1 72.3 us: local(): pl.pallas_call(coef_kernel, out_shape=(pltpu.VMEM((2, DEPTH, CY, CX), f32...]
where the time goes in v2:
time: 75.2 us; the launch traced here: 75.1 us
  Pallas kernels  75.1 us (100%)
    pallas_call x1, Pallas kernels, local(): pl.pallas_call(coef_kernel, out_shape=(pltpu.VMEM((2, DEPTH, CY, CX), f32...  72.3 us
    pallas_call x1, Pallas kernels, local(): pl.pallas_call(force_kernel, out_shape=jax.ShapeDtypeStruct((3, 2, DEPTH,...  2.81 us

profile of v2, /device:TPU:16, one launch (start us, length us, event | category | flops | bytes accessed | tf_op | source)
XLA Modules:
  0.0 75.1 jit_solution(12259051920093005376)
XLA Ops:
  0.0 72.3 %coefs.1 = (f32[2,32,64,128]{3,2,1,0:T(8,128)S(1)}, f32[3,2,32,64,128]{4,3,2,1,0:T(8,128)S(1)}) custom-call(f32[2,32,64,128]{3,2,1,0:T(8,128)} %images.1), custom_call_target="tpu_custom_call" | custom-call | tf_op jit(solution)/shard_map/coefs/pallas_call | solution.py:330
  72.3 2.8 %forces.1 = f32[3,2,32,64,128]{4,3,2,1,0:T(8,128)} custom-call(f32[2,32,64,128]{3,2,1,0:T(8,128)S(1)} %get-tuple-element.7.coef, f32[3,2,32,64,128]{4,3,2,1,0:T(8,128)S(1)} %get-tuple-element.8.gradient), custom_call_target="tpu_custom_call" | custom-call | tf_op jit(solution)/shard_map/forces/pallas_call | solution.py:354

commit v3 on v2

--- a/solution.py
+++ b/solution.py
@@ -16,9 +16,9 @@
 DEPTH = 32
 SENT = {(1, 1): 0, (2, 1): 3, (1, 0): 4, (2, 0): 7}
 RELAY = 6
-BLOCKS = ((0, 7, 20), (7, 8, 24), (15, 4, 27), (19, 4, 30))
+BLOCKS = ((0, 7, 20), (7, 8, 24), (15, 4, 26), (19, 4, 30))
 LAST = 23
-STORE = 4
+STORES = ((0, 6), (6, 6), (12, 6), (18, 5))
 LAG = 4
 
 
@@ -81,8 +81,13 @@
                 )
 
 
+def places(side):
+    from_x, from_y = 4 - 4 * side, 4 * side
+    return (2 + side, 3 - side, from_x + side, from_x + 1 - side, from_y + side, from_y + 1 - side)
+
+
 def coef_kernel(
-    images, coef_ref, gradient_ref, buf, padded, partial, operand, band, windows,
+    images, coef_ref, gradient_ref, buf, windows, padded, partial, operand, band,
     x_send, x_recv, y_send, y_recv, rim_send, rim_recv, relay_send, relay_recv, local_sem, relay,
 ):
     phase, slab = lax.axis_index("phase"), lax.axis_index("slab")
@@ -120,7 +125,7 @@
         pl.semaphore_wait(barrier, 5)
 
     from_x, from_y = 4 - 4 * side, 4 * side
-    place = (2 + side, 3 - side, from_x + side, from_x + 1 - side, from_y + side, from_y + 1 - side)
+    place = places(side)
 
     def plane_of(k):
         return (k + DEPTH - 4) % DEPTH
@@ -273,8 +278,6 @@
             @pl.when(u == step)
             def _():
                 coefs_of(first, size)
-
-    coefs_of(LAST, DEPTH - LAST)
 
     @pl.loop(0, DEPTH)
     def _(k):
@@ -303,63 +306,62 @@
         gradient_ref[2, p, z] = up - down
 
 
-def force_kernel(coef, gradient, out_ref, out, sem):
-    def copy(c):
-        planes = pl.ds(c * STORE, STORE)
-        return pltpu.make_async_copy(out.at[:, :, planes], out_ref.at[:, :, planes], sem.at[c])
-
-    @pl.loop(0, DEPTH // STORE)
-    def _(c):
-        @pl.loop(0, STORE)
-        def _(q):
-            z = c * STORE + q
+def force_kernel(coef, gradient, buf, windows, out_ref, late, out, sem):
+    def store(i, first, size, coefs):
+        @pl.loop(first, first + size)
+        def _(z):
             for p in range(2):
                 for k in range(3):
-                    out[k, p, z] = coef[p, z] * gradient[k, p, z]
-
-        copy(c).start()
-
-    @pl.loop(0, DEPTH // STORE)
-    def _(c):
-        copy(c).wait()
+                    out[k, p, z] = coefs[p, z] * gradient[k, p, z]
+
+        planes = pl.ds(first, size)
+        copy = pltpu.make_async_copy(out.at[:, :, planes], out_ref.at[:, :, planes], sem.at[i])
+        copy.start()
+        return copy
+
+    copies = [store(i, first, size, coef) for i, (first, size) in enumerate(STORES)]
+    block_coefs(LAST, DEPTH - LAST, places(lax.axis_index("phase") % 2), buf, windows, late)
+    copies.append(store(len(STORES), LAST, DEPTH - LAST, late))
+    for copy in copies:
+        copy.wait()
 
 
 def local(images):
     f32, vmem = jnp.float32, pl.BlockSpec(memory_space=pltpu.VMEM)
     dma = pltpu.SemaphoreType.DMA
-    coefs, gradient = pl.pallas_call(
+    results = pl.pallas_call(
         coef_kernel,
         out_shape=(
             pltpu.VMEM((2, DEPTH, CY, CX), f32),
             pltpu.VMEM((3, 2, DEPTH, CY, CX), f32),
+            pltpu.VMEM((6, DEPTH + 8, CY, CX), f32),
+            pltpu.VMEM((DEPTH + 8, FIELDS * CY, CX), f32),
         ),
         in_specs=[pl.BlockSpec(memory_space=pltpu.HBM)],
-        out_specs=(vmem, vmem),
+        out_specs=(vmem,) * 4,
         scratch_shapes=[
-            pltpu.VMEM((6, DEPTH + 8, CY, CX), f32),
             pltpu.VMEM((FIELDS, 80, CX), f32),
             pltpu.VMEM((FIELDS, 72, CX), f32),
             pltpu.VMEM((FIELDS * CY, 384), jnp.bfloat16),
             pltpu.VMEM((384, CX), jnp.bfloat16),
-            pltpu.VMEM((DEPTH + 8, FIELDS * CY, CX), f32),
             dma((DEPTH,)), dma((DEPTH,)), dma((DEPTH,)), dma((DEPTH,)),
             dma((3, 2)), dma((3, 2)), dma((3,)), dma, dma,
             pltpu.VMEM((2, 4, CY, CX), f32),
         ],
         compiler_params=pltpu.CompilerParams(
-            collective_id=0, has_side_effects=True, vmem_limit_bytes=54 * 2**20
+            collective_id=0, has_side_effects=True, vmem_limit_bytes=20 * 2**20
         ),
         name="coefs",
     )(images)
     return pl.pallas_call(
         force_kernel,
         out_shape=jax.ShapeDtypeStruct((3, 2, DEPTH, CY, CX), f32),
-        in_specs=[vmem, vmem],
+        in_specs=[vmem] * 4,
         out_specs=pl.BlockSpec(memory_space=pl.ANY),
-        scratch_shapes=[pltpu.VMEM((3, 2, DEPTH, CY, CX), f32), dma((DEPTH // STORE,))],
-        compiler_params=pltpu.CompilerParams(vmem_limit_bytes=16 * 2**20),
+        scratch_shapes=[pltpu.VMEM((2, DEPTH, CY, CX), f32), pltpu.VMEM((3, 2, DEPTH, CY, CX), f32), dma((len(STORES) + 1,))],
+        compiler_params=pltpu.CompilerParams(vmem_limit_bytes=10 * 2**20),
         name="forces",
-    )(coefs, gradient)
+    )(*results)
 
 
 def solution(mesh):

time: 75.2 us -> 74.2 us (0.987)
  Pallas kernels: 75.1 us -> 74 us
    pallas_call x1, Pallas kernels: 72.3 us -> 69.1 us  [local(): pl.pallas_call(coef_kernel, out_shape=(pltpu.VMEM((2, DEPTH, CY, CX), f32...]
    pallas_call x1, Pallas kernels: 2.81 us -> 4.9 us  [local(): pl.pallas_call(force_kernel, out_shape=jax.ShapeDtypeStruct((3, 2, DEPTH,...]
where the time goes in v3:
time: 74.2 us; the launch traced here: 74 us
  Pallas kernels  74 us (100%)
    pallas_call x1, Pallas kernels, local(): pl.pallas_call(coef_kernel, out_shape=(pltpu.VMEM((2, DEPTH, CY, CX), f32...  69.1 us
    pallas_call x1, Pallas kernels, local(): pl.pallas_call(force_kernel, out_shape=jax.ShapeDtypeStruct((3, 2, DEPTH,...  4.9 us

profile of v3, /device:TPU:16, one launch (start us, length us, event | category | flops | bytes accessed | tf_op | source)
XLA Modules:
  0.0 74.0 jit_solution(1927973242890915552)
XLA Ops:
  0.0 69.1 %coefs.1 = (f32[2,32,64,128]{3,2,1,0:T(8,128)S(1)}, f32[3,2,32,64,128]{4,3,2,1,0:T(8,128)S(1)}, f32[6,40,64,128]{3,2,1,0:T(8,128)S(1)}, f32[40,1216,128]{2,1,0:T(8,128)S(1)}) custom-call(f32[2,32,64,128]{3,2,1,0:T(8,128)} %images.1), custom_call_target="tpu_custom_call" | custom-call | tf_op jit(solution)/shard_map/coefs/pallas_call | solution.py:332
  69.2 4.9 %forces.1 = f32[3,2,32,64,128]{4,3,2,1,0:T(8,128)} custom-call(f32[2,32,64,128]{3,2,1,0:T(8,128)S(1)} %get-tuple-element.9.coef, f32[3,2,32,64,128]{4,3,2,1,0:T(8,128)S(1)} %get-tuple-element.10.gradient, f32[6,40,64,128]{3,2,1,0:T(8,128)S(1)} %get-tuple-element.11.buf, f32[40,1216,128]{2,1,0:T(8,128)S(1)} %get-tuple-element.12.windows), custom_call_target="tpu_custom_call" | custom-call | tf_op jit(solution)/shard_map/forces/pallas_call | solution.py:356

commit v4 on v3

--- a/solution.py
+++ b/solution.py
@@ -15,8 +15,8 @@
 CY, CX = 64, 128
 DEPTH = 32
 SENT = {(1, 1): 0, (2, 1): 3, (1, 0): 4, (2, 0): 7}
-RELAY = 6
-BLOCKS = ((0, 7, 20), (7, 8, 24), (15, 4, 26), (19, 4, 30))
+RELAY = 5
+BLOCKS = ((0, 7, 17), (7, 8, 22), (15, 8, 30))
 LAST = 23
 STORES = ((0, 6), (6, 6), (12, 6), (18, 5))
 LAG = 4
@@ -260,17 +260,17 @@
             def _(q):
                 plane_gradient((u - 8) * 4 + q, buf, gradient_ref)
 
-        @pl.when(u == 16)
+        @pl.when(u == 13)
         def _():
             await_rims((1, 2), 1)
 
-        @pl.when(u == 20)
+        @pl.when(u == 17)
         def _():
             await_rims((1, 2), 0)
 
-        @pl.when((u >= 16) & (u < 24))
-        def _():
-            at = u - 16 + DEPTH * ((u - 16) // 4)
+        @pl.when((u >= 13) & (u < 21))
+        def _():
+            at = u - 13 + DEPTH * ((u - 13) // 4)
             work(SOON, at)
             work(LATE, at)
 

time: 74.2 us -> 74.3 us (level); the launches traced: 74 us -> 73.4 us
  no operation moved by 1% of the time
where the time goes in v4:
time: 74.3 us; the launch traced here: 73.4 us
  Pallas kernels  73.4 us (99%)
    pallas_call x1, Pallas kernels, local(): pl.pallas_call(coef_kernel, out_shape=(pltpu.VMEM((2, DEPTH, CY, CX), f32...  68.5 us
    pallas_call x1, Pallas kernels, local(): pl.pallas_call(force_kernel, out_shape=jax.ShapeDtypeStruct((3, 2, DEPTH,...  4.9 us

profile of v4, /device:TPU:16, one launch (start us, length us, event | category | flops | bytes accessed | tf_op | source)
XLA Modules:
  0.0 73.4 jit_solution(2340470268819514814)
XLA Ops:
  0.0 68.5 %coefs.1 = (f32[2,32,64,128]{3,2,1,0:T(8,128)S(1)}, f32[3,2,32,64,128]{4,3,2,1,0:T(8,128)S(1)}, f32[6,40,64,128]{3,2,1,0:T(8,128)S(1)}, f32[40,1216,128]{2,1,0:T(8,128)S(1)}) custom-call(f32[2,32,64,128]{3,2,1,0:T(8,128)} %images.1), custom_call_target="tpu_custom_call" | custom-call | tf_op jit(solution)/shard_map/coefs/pallas_call | solution.py:332
  68.5 4.9 %forces.1 = f32[3,2,32,64,128]{4,3,2,1,0:T(8,128)} custom-call(f32[2,32,64,128]{3,2,1,0:T(8,128)S(1)} %get-tuple-element.9.coef, f32[3,2,32,64,128]{4,3,2,1,0:T(8,128)S(1)} %get-tuple-element.10.gradient, f32[6,40,64,128]{3,2,1,0:T(8,128)S(1)} %get-tuple-element.11.buf, f32[40,1216,128]{2,1,0:T(8,128)S(1)} %get-tuple-element.12.windows), custom_call_target="tpu_custom_call" | custom-call | tf_op jit(solution)/shard_map/forces/pallas_call | solution.py:356
